TPU v7x, 768 devices: a whole 4x8x12 slice. The times are simulated.
768 devices in a mesh: az: 96 (over y, z_lo, core), rad: 8 (over x, z_hi).
Axes of the slice: x: 4, y: 8, z: 12 (z_hi: 2, z_lo: 6; z = z_hi * 6 + z_lo), core: 2. Of those that a mesh axis runs over, the one named last changes fastest.
Arguments:
- density: float32 [4, 1536, 1024], P(None, 'az', 'rad'), may hold values from 1 to 2
- momentum: float32 [3, 4, 1536, 1024], P(None, None, 'az', 'rad'), may hold values from -2.5 to 2.5
- magnetic: float32 [3, 4, 1536, 1024], P(None, None, 'az', 'rad'), may hold values from -3 to 3
- tracer: float32 [4, 1536, 1024], P(None, 'az', 'rad'), may hold values from 0 to 1
- shear_offset: int32 [2], replicated, may hold values from 0 to 783, as said below
Outputs:
- new_state: float32 [8, 4, 1536, 1024], P(None, None, 'az', 'rad')
Inputs may be any that keep to these rules, and one draw needn't show every extreme that they name: shear_offset[0] is below 16; shear_offset[1] is 768 plus a whole number below 16.
All inputs are finite; a program needn't handle non-finite values.
Results may differ from a plain program's by a relative error of at most 0.00002.
Values sent between devices are 32-bit elements; how exact they have to be, the bound alone decides.
A program may use at most 32 MiB of HBM per device.

v0:
```python
import jax
import jax.numpy as jnp
from jax import lax
from jax.sharding import PartitionSpec as P

time_step = 0.025
viscosity = 0.5
sound_squared = 1.0
shear_speed = 1.0
frac_weight = 0.375


def with_halo(cells, sides, width):
    for axis, dim in sides:
        count = lax.axis_size(axis)
        head = lax.slice_in_dim(cells, 0, width, axis=dim)
        tail = lax.slice_in_dim(cells, cells.shape[dim] - width, cells.shape[dim], axis=dim)
        cells = jnp.concatenate(
            [
                lax.ppermute(tail, axis, [(i, (i + 1) % count) for i in range(count)]),
                cells,
                lax.ppermute(head, axis, [((i + 1) % count, i) for i in range(count)]),
            ],
            axis=dim,
        )
    return cells


def fluxes(padded, direction):
    density_part = padded[0]
    velocity = [padded[1 + component] / density_part for component in range(3)]
    field_part = [padded[4 + component] for component in range(3)]
    pressure = sound_squared * density_part + 0.5 * (
        field_part[0] * field_part[0]
        + field_part[1] * field_part[1]
        + field_part[2] * field_part[2]
    )
    normal_vel = velocity[direction]
    normal_mag = field_part[direction]
    result = [padded[1 + direction]]
    for component in range(3):
        summand = padded[1 + component] * normal_vel - field_part[component] * normal_mag
        if component == direction:
            summand = summand + pressure
        result.append(summand)
    for component in range(3):
        result.append(normal_vel * field_part[component] - normal_mag * velocity[component])
    result.append(padded[7] * normal_vel)
    return jnp.stack(result)


def offset_slice(padded, along, length, shift_by):
    return lax.slice_in_dim(padded, 3 + shift_by, 3 + shift_by + length, axis=along)


def central(padded, along, length):
    return (
        45.0 * (offset_slice(padded, along, length, 1) - offset_slice(padded, along, length, -1))
        - 9.0 * (offset_slice(padded, along, length, 2) - offset_slice(padded, along, length, -2))
        + (offset_slice(padded, along, length, 3) - offset_slice(padded, along, length, -3))
    ) / 60.0


def second(padded, along, length):
    return (
        offset_slice(padded, along, length, 1)
        - 2.0 * offset_slice(padded, along, length, 0)
        + offset_slice(padded, along, length, -1)
    )


def tendency(row_padded, col_padded):
    row_count = row_padded.shape[2] - 6
    col_count = col_padded.shape[3] - 6
    core_rows = row_padded[:, :, 3 : 3 + row_count]
    vertical_pad = jnp.concatenate([core_rows[:, -3:], core_rows, core_rows[:, :3]], axis=1)
    layer_count = core_rows.shape[1]
    summed = -(
        central(fluxes(col_padded, 0), 3, col_count)
        + central(fluxes(row_padded, 1), 2, row_count)
        + central(fluxes(vertical_pad, 2), 1, layer_count)
    )
    summed = summed + viscosity * (
        second(col_padded, 3, col_count)
        + second(row_padded, 2, row_count)
        + second(vertical_pad, 1, layer_count)
    )
    return summed


def blend_rows(window, row_count, lead_weight, trail_weight, jump_sign):
    blended = (
        lead_weight * window[:, :, :row_count] + trail_weight * window[:, :, 1 : row_count + 1]
    )
    return jnp.concatenate(
        [blended[:2], blended[2:3] + jump_sign * shear_speed * blended[0:1], blended[3:]], axis=0
    )


def pack_pair(paired):
    return jnp.moveaxis(paired, 4, 2).reshape(paired.shape[0], paired.shape[1], paired.shape[4], -1)


def sheared(inner_src, outer_src, offset, own_rows):
    layers = inner_src.shape[1]
    src_rows = inner_src.shape[2]
    halo_rows = (src_rows - own_rows) // 2
    window_rows = own_rows + 2 * halo_rows
    total_rows = own_rows * lax.axis_size("az")
    starts = [offset, total_rows - 1 - offset]
    paired = jnp.stack([inner_src, outer_src])
    windows = []
    flat_pair = pack_pair(paired).reshape(1, -1)
    collected = lax.all_gather(flat_pair, "az", axis=0, tiled=True)
    count = collected.shape[0]
    spread = collected.reshape(count, 2, paired.shape[1], 3, layers, own_rows)
    gathered = jnp.transpose(spread, (1, 2, 4, 0, 5, 3)).reshape(
        2, paired.shape[1], layers, count * own_rows, 3
    )
    extended = jnp.concatenate([gathered, gathered[:, :, :, : window_rows + 1]], axis=3)
    first_row = lax.axis_index("az") * own_rows - halo_rows
    for side_index in range(2):
        windows.append(
            lax.dynamic_slice_in_dim(
                extended[side_index],
                (first_row + starts[side_index]) % total_rows,
                window_rows + 1,
                2,
            )
        )
    inner_ghost = blend_rows(windows[0], window_rows, 1.0 - frac_weight, frac_weight, 1.0)
    outer_ghost = blend_rows(windows[1], window_rows, frac_weight, 1.0 - frac_weight, -1.0)
    return (inner_ghost, outer_ghost)


def radial_pad(source, offset, own_rows):
    layers = source.shape[1]
    rows = source.shape[2]
    edges = jnp.concatenate([source[..., :3], source[..., -3:]], axis=3)
    flat_edges = jnp.moveaxis(edges, 3, 1).reshape(source.shape[0], 6, -1)
    arrived = with_halo(flat_edges, (("rad", 1),), 3)
    columns = jnp.moveaxis(arrived.reshape(source.shape[0], 12, layers, rows), 1, 3)
    inner_src = columns[..., :3]
    outer_src = columns[..., -3:]
    inner_ghost, outer_ghost = sheared(inner_src, outer_src, offset, own_rows)
    position = lax.axis_index("rad")
    last_index = lax.axis_size("rad") - 1
    left_cols = jnp.where(position == 0, inner_ghost, inner_src)
    right_cols = jnp.where(position == last_index, outer_ghost, outer_src)
    return jnp.concatenate([left_cols, source, right_cols], axis=3)


def shards(density, momentum, magnetic, tracer, shear_offset):
    conserved = jnp.concatenate([density[None], momentum, magnetic, tracer[None]], axis=0)
    own_rows = conserved.shape[2]
    current = conserved
    for section_index in range(2):
        row_padded = with_halo(current, (("az", 2),), 3)
        current = current + time_step * tendency(
            row_padded, radial_pad(current, shear_offset[section_index], own_rows)
        )
    return 0.5 * conserved + 0.5 * current


def solution(mesh):
    placed = (
        P(None, "az", "rad"),
        P(None, None, "az", "rad"),
        P(None, None, "az", "rad"),
        P(None, "az", "rad"),
        P(),
    )
    return jax.shard_map(
        shards, mesh=mesh, in_specs=placed, out_specs=P(None, None, "az", "rad"), check_vma=False
    )
```

profile of v0, /device:TPU:1, one launch (start us, length us, event | category | flops | bytes accessed | tf_op | source)
XLA Modules:
  0.0 456.8 jit_solution(15859827141671225554)
XLA Ops:
  6.5 1.0 pad_maximum_fusion.36
  7.5 0.1 fusion.71
  7.7 0.3 copy.298
  8.0 0.3 copy.299
  8.3 0.1 reshape.32
  8.4 15.7 %collective-permute-start = (f32[8,3,64]{2,0,1:T(8,128)S(1)}, f32[8,3,64]{2,0,1:T(8,128)S(1)}, u32[]{:S(2)}, u32[]{:S(2)}) collective-permute-start(f32[8,3,64]{2,0,1:T(8,128)S(1)} %get-tuple-element.39), channel_id=1, source_target_pairs={{0,1},{1,2},{2,3},{3,4},{4,5},{5,6},{6,7},{7,0},{8,9},{9,10},{10,1... | collective-permute-start | bytes 18440 | tf_op jit(solution)/shard_map/ppermute | solution.py:20
  24.1 4.1 collective-permute-start.1
  28.3 3.9 collective-permute-start.2
  32.3 4.8 %collective-permute-start.3 = (f32[8,4,3,128]{3,0,2,1:T(8,128)S(1)}, f32[8,4,3,128]{3,0,2,1:T(8,128)S(1)}, u32[]{:S(2)}, u32[]{:S(2)}) collective-permute-start(f32[8,4,3,128]{3,0,2,1:T(8,128)S(1)} %copy.335), channel_id=1, source_target_pairs={{8,0},{16,8},{24,16},{32,24},{40,32},{48,40},{56,48},{64,56},{72,6... | collective-permute-start | bytes 147464 | tf_op jit(solution)/shard_map/ppermute | solution.py:22
  37.2 0.7 copy-done.7
  38.2 0.1 concatenate.99
  38.3 0.1 concatenate.100
  38.5 0.7 reshape.38
  39.4 0.7 fusion.76
  43.0 171.5 %all-gather.5.cloned.1.call-done = f32[96,1,3072]{2,1,0:T(1,128)} async-done(((f32[1,1,3072]{2,1,0:T(1,128)}), f32[96,1,3072]{2,1,0:T(1,128)}) %all-gather.5.cloned.1.call-update) | async-done | bytes 1179664 | tf_op jit(solution)/shard_map/all_gather | solution.py:114
  214.5 2.5 copy.304
  216.9 5.1 %copy.305 = f32[2,8,4,96,16,3]{4,3,1,5,2,0:T(8,128)} copy(f32[2,8,4,96,16,3]{3,4,2,5,1,0:T(8,128)S(1)} %bitcast.58) | data formatting | bytes 2359296 | tf_op jit(solution)/shard_map/transpose | solution.py:117
  222.0 8.4 %reshape.34 = f32[2,8,4,1536,3]{3,1,4,2,0:T(8,128)S(1)} reshape(f32[2,8,4,96,16,3]{4,3,1,5,2,0:T(8,128)} %copy.305) | data formatting | bytes 2359296 | tf_op jit(solution)/shard_map/reshape | solution.py:117
  230.6 0.1 fusion.65
  230.8 0.1 fusion.57
  231.1 0.3 copy.306
  231.4 0.3 copy.307
  231.6 0.3 pad_maximum_fusion.2
  232.1 0.8 copy-done.1
  233.1 0.7 fusion.34
  233.8 0.1 fusion.68
  234.0 0.3 copy.316
  234.3 0.3 copy.317
  234.6 0.1 reshape.35
  234.7 8.1 %collective-permute-start.4 = (f32[8,3,64]{2,0,1:T(8,128)S(1)}, f32[8,3,64]{2,0,1:T(8,128)S(1)}, u32[]{:S(2)}, u32[]{:S(2)}) collective-permute-start(f32[8,3,64]{2,0,1:T(8,128)S(1)} %get-tuple-element.37), channel_id=1, source_target_pairs={{0,1},{1,2},{2,3},{3,4},{4,5},{5,6},{6,7},{7,0},{8,9},{9,10},{10,1... | collective-permute-start | bytes 18440 | tf_op jit(solution)/shard_map/ppermute | solution.py:20
  242.8 5.6 %collective-permute-start.5 = (f32[8,3,64]{2,0,1:T(8,128)S(1)}, f32[8,3,64]{2,0,1:T(8,128)S(1)}, u32[]{:S(2)}, u32[]{:S(2)}) collective-permute-start(f32[8,3,64]{2,0,1:T(8,128)S(1)} %get-tuple-element.38), channel_id=1, source_target_pairs={{1,0},{2,1},{3,2},{4,3},{5,4},{6,5},{7,6},{0,7},{9,8},{10,9},{11,1... | collective-permute-start | bytes 18440 | tf_op jit(solution)/shard_map/ppermute | solution.py:22
  248.5 4.3 collective-permute-start.6
  252.8 2.1 collective-permute-start.7
  255.2 0.1 concatenate.115
  255.3 0.1 concatenate.116
  255.5 0.7 reshape.40
  256.3 1.9 collective-permute-done.7
  258.5 171.4 %all-gather.7.cloned.1.call-done = f32[96,1,3072]{2,1,0:T(1,128)} async-done(((f32[1,1,3072]{2,1,0:T(1,128)}), f32[96,1,3072]{2,1,0:T(1,128)}) %all-gather.7.cloned.1.call-update) | async-done | bytes 1179664 | tf_op jit(solution)/shard_map/all_gather | solution.py:114
  429.8 2.5 copy.322
  432.3 5.1 %copy.323 = f32[2,8,4,96,16,3]{4,3,1,5,2,0:T(8,128)} copy(f32[2,8,4,96,16,3]{3,4,2,5,1,0:T(8,128)S(1)} %bitcast.59) | data formatting | bytes 2359296 | tf_op jit(solution)/shard_map/transpose | solution.py:117
  437.4 8.4 %reshape.37 = f32[2,8,4,1536,3]{3,1,4,2,0:T(8,128)S(1)} reshape(f32[2,8,4,96,16,3]{4,3,1,5,2,0:T(8,128)} %copy.323) | data formatting | bytes 2359296 | tf_op jit(solution)/shard_map/reshape | solution.py:117
  445.9 0.1 fusion.62
  446.2 0.1 fusion.59
  446.5 0.3 copy.324
  446.7 0.3 copy.325
  447.0 0.3 pad_maximum_fusion.3
  447.6 0.8 copy-done.3
  448.5 1.4 fusion.7
  (151 shorter events, 2.9 us)
Async XLA Ops:
  6.5 207.9 %all-gather.5.cloned.1.call-start = ((), (), s32[]{:S(2)}) async-start(), calls=%async_computation | async-start | bytes 1191936 | tf_op jit(solution)/shard_map/all_gather | solution.py:114
  7.7 30.2 %copy-start.4 = (f32[3,4,16,128]{3,2,1,0:T(8,128)S(1)}, f32[3,4,16,128]{3,2,1,0:T(8,128)}, u32[]{:S(2)}) copy-start(f32[3,4,16,128]{3,2,1,0:T(8,128)} %param.7) | copy-start | bytes 294916
  7.7 30.2 %copy-start.5 = (f32[3,4,16,128]{3,2,1,0:T(8,128)S(1)}, f32[3,4,16,128]{3,2,1,0:T(8,128)}, u32[]{:S(2)}) copy-start(f32[3,4,16,128]{3,2,1,0:T(8,128)} %param.6) | copy-start | bytes 294916
  7.7 30.2 %copy-start.15 = (f32[4,16,128]{2,1,0:T(8,128)S(1)}, f32[4,16,128]{2,1,0:T(8,128)}, u32[]{:S(2)}) copy-start(f32[4,16,128]{2,1,0:T(8,128)} %param.8) | copy-start | bytes 98308
  7.7 30.2 %copy-start.16 = (f32[4,16,128]{2,1,0:T(8,128)S(1)}, f32[4,16,128]{2,1,0:T(8,128)}, u32[]{:S(2)}) copy-start(f32[4,16,128]{2,1,0:T(8,128)} %param.5) | copy-start | bytes 98308
  8.4 29.8 %collective-permute-start = (f32[8,3,64]{2,0,1:T(8,128)S(1)}, f32[8,3,64]{2,0,1:T(8,128)S(1)}, u32[]{:S(2)}, u32[]{:S(2)}) collective-permute-start(f32[8,3,64]{2,0,1:T(8,128)S(1)} %get-tuple-element.39), channel_id=1, source_target_pairs={{0,1},{1,2},{2,3},{3,4},{4,5},{5,6},{6,7},{7,0},{8,9},{9,10},{10,1... | collective-permute-start | bytes 18440 | tf_op jit(solution)/shard_map/ppermute | solution.py:20
  24.1 14.2 %collective-permute-start.1 = (f32[8,3,64]{2,0,1:T(8,128)S(1)}, f32[8,3,64]{2,0,1:T(8,128)S(1)}, u32[]{:S(2)}, u32[]{:S(2)}) collective-permute-start(f32[8,3,64]{2,0,1:T(8,128)S(1)} %get-tuple-element.40), channel_id=1, source_target_pairs={{1,0},{2,1},{3,2},{4,3},{5,4},{6,5},{7,6},{0,7},{9,8},{10,9},{11,1... | collective-permute-start | bytes 18440 | tf_op jit(solution)/shard_map/ppermute | solution.py:22
  28.3 14.4 %collective-permute-start.2 = (f32[8,4,3,128]{3,0,2,1:T(8,128)S(1)}, f32[8,4,3,128]{3,0,2,1:T(8,128)S(1)}, u32[]{:S(2)}, u32[]{:S(2)}) collective-permute-start(f32[8,4,3,128]{3,0,2,1:T(8,128)S(1)} %copy.334), channel_id=1, source_target_pairs={{0,8},{8,16},{16,24},{24,32},{32,40},{40,48},{48,56},{56,64},{64,7... | collective-permute-start | bytes 147464 | tf_op jit(solution)/shard_map/ppermute | solution.py:20
  32.3 10.4 %collective-permute-start.3 = (f32[8,4,3,128]{3,0,2,1:T(8,128)S(1)}, f32[8,4,3,128]{3,0,2,1:T(8,128)S(1)}, u32[]{:S(2)}, u32[]{:S(2)}) collective-permute-start(f32[8,4,3,128]{3,0,2,1:T(8,128)S(1)} %copy.335), channel_id=1, source_target_pairs={{8,0},{16,8},{24,16},{32,24},{40,32},{48,40},{56,48},{64,56},{72,6... | collective-permute-start | bytes 147464 | tf_op jit(solution)/shard_map/ppermute | solution.py:22
  37.2 0.7 copy-start.7
  37.2 0.7 copy-start.9
  38.1 1.2 copy-start.18
  39.3 390.6 %all-gather.7.cloned.1.call-start = ((), (), s32[]{:S(2)}) async-start(), calls=%async_computation.1 | async-start | bytes 1191936 | tf_op jit(solution)/shard_map/all_gather | solution.py:114
  39.4 3.4 copy-start
  231.9 1.1 copy-start.1
  231.9 1.1 copy-start.8
  231.9 1.2 copy-start.10
  234.0 20.9 %copy-start.11 = (f32[8,3,16,128]{3,2,1,0:T(8,128)}, f32[8,3,16,128]{3,2,1,0:T(8,128)S(1)}, u32[]{:S(2)}) copy-start(f32[8,3,16,128]{3,2,1,0:T(8,128)S(1)} %get-tuple-element.21) | copy-start | bytes 589828
  234.0 20.9 %copy-start.13 = (f32[8,3,16,128]{3,2,1,0:T(8,128)}, f32[8,3,16,128]{3,2,1,0:T(8,128)S(1)}, u32[]{:S(2)}) copy-start(f32[8,3,16,128]{3,2,1,0:T(8,128)S(1)} %get-tuple-element.22) | copy-start | bytes 589828
  234.7 20.5 %collective-permute-start.4 = (f32[8,3,64]{2,0,1:T(8,128)S(1)}, f32[8,3,64]{2,0,1:T(8,128)S(1)}, u32[]{:S(2)}, u32[]{:S(2)}) collective-permute-start(f32[8,3,64]{2,0,1:T(8,128)S(1)} %get-tuple-element.37), channel_id=1, source_target_pairs={{0,1},{1,2},{2,3},{3,4},{4,5},{5,6},{6,7},{7,0},{8,9},{9,10},{10,1... | collective-permute-start | bytes 18440 | tf_op jit(solution)/shard_map/ppermute | solution.py:20
  242.8 12.5 %collective-permute-start.5 = (f32[8,3,64]{2,0,1:T(8,128)S(1)}, f32[8,3,64]{2,0,1:T(8,128)S(1)}, u32[]{:S(2)}, u32[]{:S(2)}) collective-permute-start(f32[8,3,64]{2,0,1:T(8,128)S(1)} %get-tuple-element.38), channel_id=1, source_target_pairs={{1,0},{2,1},{3,2},{4,3},{5,4},{6,5},{7,6},{0,7},{9,8},{10,9},{11,1... | collective-permute-start | bytes 18440 | tf_op jit(solution)/shard_map/ppermute | solution.py:22
  248.5 7.8 %collective-permute-start.6 = (f32[8,4,3,128]{3,0,2,1:T(8,128)S(1)}, f32[8,4,3,128]{3,0,2,1:T(8,128)S(1)}, u32[]{:S(2)}, u32[]{:S(2)}) collective-permute-start(f32[8,4,3,128]{3,0,2,1:T(8,128)S(1)} %copy.326), channel_id=1, source_target_pairs={{0,8},{8,16},{16,24},{24,32},{32,40},{40,48},{48,56},{56,64},{64,7... | collective-permute-start | bytes 147464 | tf_op jit(solution)/shard_map/ppermute | solution.py:20
  252.8 5.4 %collective-permute-start.7 = (f32[8,4,3,128]{3,0,2,1:T(8,128)S(1)}, f32[8,4,3,128]{3,0,2,1:T(8,128)S(1)}, u32[]{:S(2)}, u32[]{:S(2)}) collective-permute-start(f32[8,4,3,128]{3,0,2,1:T(8,128)S(1)} %copy.327), channel_id=1, source_target_pairs={{8,0},{16,8},{24,16},{32,24},{40,32},{48,40},{56,48},{64,56},{72,6... | collective-permute-start | bytes 147464 | tf_op jit(solution)/shard_map/ppermute | solution.py:22
  256.3 1.9 copy-start.2
  447.3 1.1 copy-start.3
  447.3 1.1 copy-start.6
  447.3 1.1 copy-start.12
  447.3 1.2 copy-start.14
  447.3 1.2 copy-start.17
Sparse Core Ops, SparseCore 0:
  39.4 175.0 all-gather.4
  256.4 173.4 all-gather.6
where the time goes:
time: 457 us
  waiting for transfers between devices  345 us (75%)
  starting transfers between devices  48.7 us (11%)
  local copies, waits for them, and re-layouts  40.4 us (9%)
  between operations  17.2 us (4%)
  other arithmetic  5.71 us (1%)
    all_gather x2, waiting for transfers between devices, sheared(): collected = lax.all_gather(flat_pair, 'az', axis=0, tiled=True)  343 us
    ppermute x4, starting transfers between devices, with_halo(): lax.ppermute(tail, axis, [(i, (i + 1) % count) for i in range(count)])  32 us
    reshape x2, local copies, waits for them, and re-layouts, sheared(): jnp.transpose(spread, (1, 2, 4, 0, 5, 3))  16.8 us
    ppermute x4, starting transfers between devices, with_halo(): lax.ppermute(head, axis, [((i + 1) % count, i) for i in range(count)])  16.7 us
    transpose x2, local copies, waits for them, and re-layouts, sheared(): jnp.transpose(spread, (1, 2, 4, 0, 5, 3))  10.2 us
  transfers between devices with their start and end apart: 10, of which 3 were waited for; matrix products, arithmetic and copies ran while one was open for 1% of the time, Pallas kernels for 0%

commit v1 on v0

v1 whole, which is shorter than its diff:
```python
import functools

import jax
import jax.numpy as jnp
from jax import lax
from jax.experimental import pallas as pl
from jax.experimental.pallas import tpu as pltpu
from jax.sharding import PartitionSpec as P

time_step = 0.025
viscosity = 0.5
sound_squared = 1.0
shear_speed = 1.0
frac_weight = 0.375

MESH = pl.DeviceIdType.MESH
D1 = -time_step * 45.0 / 60.0
D2 = time_step * 9.0 / 60.0
D3 = -time_step / 60.0
VISC = time_step * viscosity
lead = 1.0 - frac_weight
trail = frac_weight

Y_PREV, Y_NEXT, HL_MAIN, HL_PREV, HL_NEXT, HL_FULL, HR_MAIN, HR_NEXT, HR_PREV, HR_FULL, AZ_PREV, AZ_NEXT, SWAP = range(13)
N_COPY = 13


def flux(q, inv, pres, d):
    vel = [q[1 + i] * inv for i in range(3)]
    mag = q[4:7]
    vd, bd = vel[d], mag[d]
    out = [q[1 + d]]
    for i in range(3):
        g = q[1 + i] * vd - mag[i] * bd
        out.append(g + pres if i == d else g)
    for i in range(3):
        out.append(vd * mag[i] - bd * vel[i])
    out.append(q[7] * vd)
    return out


def aux(q):
    inv = 1.0 / q[0]
    pres = sound_squared * q[0] + 0.5 * (q[4] * q[4] + q[5] * q[5] + q[6] * q[6])
    return inv, pres


def combine(up, down):
    return D1 * (up[0] - down[0]) + D2 * (up[1] - down[1]) + D3 * (up[2] - down[2])


def lane_roll(x, shift):
    shift %= 128
    return x if shift == 0 else pltpu.roll(x, shift, x.ndim - 1)


def lanes_along(g, u):
    r = combine([lane_roll(g, -k) for k in (1, 2, 3)], [lane_roll(g, k) for k in (1, 2, 3)])
    return r + VISC * (lane_roll(u, -1) - 2.0 * u + lane_roll(u, 1))


def around(x, k):
    k %= x.shape[0]
    return x if k == 0 else jnp.concatenate([x[k:], x[:k]], axis=0)


def layers_along(g, u):
    r = combine([around(g, k) for k in (1, 2, 3)], [around(g, -k) for k in (1, 2, 3)])
    return r + VISC * (around(u, 1) - 2.0 * u + around(u, -1))


def lane_layers_along(g, u):
    r = combine([lane_roll(g, -32 * k) for k in (1, 2, 3)], [lane_roll(g, 32 * k) for k in (1, 2, 3)])
    return r + VISC * (lane_roll(u, -32) - 2.0 * u + lane_roll(u, 32))


def kernel(n_az, n_rad, half_offset, off_ref, den, mom, mag, tra, out,
           w, fy, own, bhl, bhr, az, es, sp, sq, in_sem, send, recv):
    a = lax.axis_index("az")
    r = lax.axis_index("rad")
    first = r == 0
    last = r == n_rad - 1
    edge = jnp.logical_or(first, last)
    r_up = lax.rem(r + 1, n_rad)
    r_dn = lax.rem(r + n_rad - 1, n_rad)

    def at(step):
        return lax.rem(a + step + n_az, n_az)

    def dev(step, to_r):
        return (at(step), to_r)

    barrier = pltpu.get_barrier_semaphore()

    def greet(step, to_r):
        pl.semaphore_signal(barrier, inc=1, device_id=dev(step, to_r), device_id_type=MESH)

    for step in (-1, 0, 1):
        greet(step, r_up)
        greet(step, r_dn)

    @pl.when(first)
    def _():
        greet(2, r_dn)

    @pl.when(last)
    def _():
        greet(-2, r_up)

    @pl.when(edge)
    def _():
        greet(n_az // 2, r)

    greet(1, r)
    greet(-1, r)

    rows = pl.ds(8, 16)
    loads = [
        pltpu.make_async_copy(den, w.at[0, :, rows], in_sem.at[0]),
        pltpu.make_async_copy(mom, w.at[1:4, :, rows], in_sem.at[1]),
        pltpu.make_async_copy(mag, w.at[4:7, :, rows], in_sem.at[2]),
        pltpu.make_async_copy(tra, w.at[7, :, rows], in_sem.at[3]),
    ]
    for c in loads:
        c.start()
    w[:, :, 0:2, :] = jnp.ones((8, 4, 2, 128), jnp.float32)
    w[:, :, 30:32, :] = jnp.ones((8, 4, 2, 128), jnp.float32)
    for c in loads:
        c.wait()

    lane = lax.broadcasted_iota(jnp.int32, (1, 128), 1)
    group = lane // 4
    slot_is = [lane % 32 // 4 == k for k in range(8)]
    left_half = lane % 32 < 16

    def pack(read, count):
        tiles = [jnp.zeros((count, 128), jnp.float32)] * 4
        for f in range(8):
            x = read(f)
            for z in range(4):
                moved = lane_roll(x[z], 32 * z + 4 * f)
                for t, shift in enumerate((0, 1, -1, -2)):
                    here = group == (8 * z + f + shift) % 32
                    tiles[t] = jnp.where(here, moved, tiles[t])
        return tiles

    def spread(f, hlf, hln, ln, lf, rf, rn, hrn, hrf):
        def of(k):
            return slot_is[(f + k) % 8]
        left = jnp.where(of(-2), hlf, jnp.where(of(-1), hln, jnp.where(of(0), ln, lf)))
        right = jnp.where(of(-2), rf, jnp.where(of(-1), rn, jnp.where(of(0), hrn, hrf)))
        return jnp.where(left_half, lane_roll(left, 4 * (2 - f)), lane_roll(right, 4 * (6 - f)))

    tiles = pack(lambda f: w[f, :, 8:24, :], 16)
    for t in range(4):
        own[t, 8:24, :] = tiles[t]
    az[24:40, :] = jnp.where(first, tiles[0], tiles[2])

    pl.semaphore_wait(barrier, 8 + 2 * edge.astype(jnp.int32))

    def remote(k, src, dst, step, to_r):
        return pltpu.make_async_remote_copy(
            src_ref=src, dst_ref=dst, send_sem=send.at[k], recv_sem=recv.at[k],
            device_id=dev(step, to_r), device_id_type=MESH)

    own_l, own_r = own.at[0:2, 8:24], own.at[2:4, 8:24]
    ln, rn = own.at[0], own.at[2]
    hl_main = remote(HL_MAIN, own_r, bhl.at[:, 8:24], 0, r_up)
    hr_main = remote(HR_MAIN, own_l, bhr.at[:, 24:40], 0, r_dn)
    hl_full = remote(HL_FULL, own_r, bhl.at[:, 24:40], -1, r_up)
    hr_full = remote(HR_FULL, own_l, bhr.at[:, 8:24], 1, r_dn)
    hl_prev = remote(HL_PREV, rn.at[21:24], bhl.at[0, 5:8], 1, r_up)
    hr_next = remote(HR_NEXT, ln.at[8:11], bhr.at[0, 40:43], -1, r_dn)
    hl_next_in = remote(HL_NEXT, rn.at[8:11], bhl.at[0, 24:27], -1, r_up)
    hl_next_end = remote(HL_NEXT, rn.at[8:11], bhl.at[0, 40:43], -2, r_up)
    hr_prev_in = remote(HR_PREV, ln.at[21:24], bhr.at[0, 21:24], 1, r_dn)
    hr_prev_end = remote(HR_PREV, ln.at[21:24], bhr.at[0, 5:8], 2, r_dn)
    az_prev = remote(AZ_PREV, az.at[24:40], az.at[8:24], 1, r)
    az_next = remote(AZ_NEXT, az.at[24:40], az.at[40:56], -1, r)
    y_prev = remote(Y_PREV, w.at[:, :, 18:24], w.at[:, :, 2:8], 1, r)
    y_next = remote(Y_NEXT, w.at[:, :, 8:14], w.at[:, :, 24:30], -1, r)
    swap = remote(SWAP, sp, sq, n_az // 2, r)

    hl_main.start()
    hr_main.start()

    @pl.when(last)
    def _():
        hl_full.start()
        hl_next_end.start()

    @pl.when(jnp.logical_not(last))
    def _():
        hl_next_in.start()

    @pl.when(first)
    def _():
        hr_full.start()
        hr_prev_end.start()

    @pl.when(jnp.logical_not(first))
    def _():
        hr_prev_in.start()

    hl_prev.start()
    hr_next.start()

    @pl.when(edge)
    def _():
        az_prev.start()
        az_next.start()

    y_prev.start()
    y_next.start()

    zero = jnp.int32(0)
    s_raw = jnp.clip(off_ref[0], 0, 15)
    t_raw = jnp.clip(off_ref[1] - half_offset, 0, 15)
    s_f = jnp.where(first, s_raw, zero)
    s_l = jnp.where(last, s_raw, zero)
    t_f = jnp.where(first, t_raw, zero)
    t_l = jnp.where(last, t_raw, zero)
    end_l = jnp.where(last, 1, zero)
    end_f = jnp.where(first, 1, zero)

    hl_main.wait_recv()
    hr_main.wait_recv()
    hl_prev.wait_recv()
    hr_next.wait_recv()
    hl_next_in.wait_recv()
    hr_prev_in.wait_recv()

    @pl.when(first)
    def _():
        hl_full.wait_recv()

    @pl.when(last)
    def _():
        hr_full.wait_recv()

    @pl.when(edge)
    def _():
        az_prev.wait_recv()
        az_next.wait_recv()

    def jump(fields, mask_l, mask_r):
        add = jnp.where(mask_l, shear_speed, 0.0) - jnp.where(mask_r, shear_speed, 0.0)
        fields[2] = jnp.where(jnp.logical_or(mask_l, mask_r), fields[2] + add * fields[0], fields[2])

    win = 24
    hlf = bhl[1, pl.ds(5 + t_f, win), :]
    hln = bhl[0, pl.ds(5 + t_f, win), :]
    hrf = bhr[1, pl.ds(21 - t_l - end_l, win), :]
    hrn = bhr[0, pl.ds(21 - t_l - end_l, win), :]
    o_l = 21 + t_f - s_f
    ln2 = jnp.where(first, trail * az[pl.ds(o_l - end_f, win), :] + lead * az[pl.ds(o_l, win), :], own[0, 5:29, :])
    o_r = 21 - t_l - end_l + s_l
    rn2 = jnp.where(last, lead * az[pl.ds(o_r, win), :] + trail * az[pl.ds(o_r + 1, win), :], own[2, 5:29, :])
    e = [spread(f, hlf, hln, ln2, ln2, rn2, rn2, hrn, hrf) for f in range(8)]
    cols = lane % 32
    in_l = jnp.logical_and(cols >= 8, cols < 16)
    in_r = jnp.logical_and(cols >= 16, cols < 24)
    jump(e, jnp.logical_and(last, in_r), jnp.logical_and(first, in_l))
    inv, pres = aux(e)
    gx = flux(e, inv, pres, 0)
    gy = flux(e, inv, pres, 1)
    gz = flux(e, inv, pres, 2)
    for f in range(8):
        es[f, 0:24, :] = gy[f]
    for f in range(8):
        es[8 + f, 0:24, :] = e[f]
    strip = []
    for f in range(8):
        def y(k, f=f):
            return es[f, 3 + k:20 + k, :]
        def u(k, f=f):
            return es[8 + f, 3 + k:20 + k, :]
        ty = combine([y(1), y(2), y(3)], [y(-1), y(-2), y(-3)]) + VISC * (u(1) - 2.0 * u(0) + u(-1))
        es[16 + f, 0:24, :] = e[f] + lanes_along(gx[f], e[f]) + lane_layers_along(gz[f], e[f])
        es[16 + f, 3:20, :] = es[16 + f, 3:20, :] + ty
    at_l = jnp.logical_and(first, left_half)
    at_r = jnp.logical_and(last, jnp.logical_not(left_half))
    w_0 = jnp.where(left_half, lead, trail)
    w_1 = jnp.where(left_half, trail, lead)
    sheared = jnp.logical_or(at_l, at_r)
    for f in range(8):
        here, beyond = es[16 + f, 3:19, :], es[16 + f, 4:20, :]
        strip.append(jnp.where(sheared, w_0 * here + w_1 * beyond, here))
    jump(strip, at_l, at_r)
    packed = jnp.zeros((16, 128), jnp.float32)
    for f in range(8):
        src = jnp.where(first, strip[f], lane_roll(strip[f], -20))
        packed = jnp.where(slot_is[f], lane_roll(src, 4 * (f - 1)), packed)
    sp[...] = packed

    @pl.when(edge)
    def _():
        swap.start()

    for f in range(8):
        es[16 + f, 0:16, :] = strip[f]

    y_prev.wait_recv()
    y_next.wait_recv()
    low = pack(lambda f: w[f, :, 0:8, :], 8)
    high = pack(lambda f: w[f, :, 24:32, :], 8)
    for t in range(4):
        own[t, 0:8, :] = low[t]
        own[t, 24:32, :] = high[t]
    hln0, hln1 = bhl[0, pl.ds(5 + s_f, win), :], bhl[0, pl.ds(5 + s_f + end_f, win), :]
    hln = jnp.where(first, lead * hln0 + trail * hln1, hln0)
    o_r = 21 - s_l
    hrn0, hrn1 = bhr[0, pl.ds(o_r - end_l, win), :], bhr[0, pl.ds(o_r, win), :]
    hrn = jnp.where(last, trail * hrn0 + lead * hrn1, hrn1)
    mine = [own[t, 5:29, :] for t in range(4)]
    e = [spread(f, hln, hln, mine[0], mine[1], mine[3], mine[2], hrn, hrn) for f in range(8)]
    jump(e, jnp.logical_and(first, cols < 8), jnp.logical_and(last, cols >= 24))
    inv, pres = aux(e)
    gx = flux(e, inv, pres, 0)
    edge_x = [lanes_along(gx[f], e[f]) for f in range(8)]

    at_left, at_right = lane < 3, lane >= 125

    def mend(inner, strip_f):
        fixed = []
        for z in range(4):
            from_l = lane_roll(strip_f, -(32 * z + 8))
            from_r = lane_roll(strip_f, 104 - 32 * z)
            fixed.append(jnp.where(at_left, from_l, jnp.where(at_right, from_r, inner[z])))
        return jnp.stack(fixed)

    q = [w[f] for f in range(8)]
    inv, pres = aux(q)
    gy = flux(q, inv, pres, 1)
    for f in range(8):
        fy[f] = gy[f]
    q = [w[f, :, 5:29, :] for f in range(8)]
    inv, pres = aux(q)
    gx = flux(q, inv, pres, 0)
    gz = flux(q, inv, pres, 2)
    one = []
    for f in range(8):
        def y(k, f=f):
            return fy[f, :, 5 + k:29 + k, :]
        ty = combine([y(1), y(2), y(3)], [y(-1), y(-2), y(-3)])
        ty = ty + VISC * (w[f, :, 6:30, :] - 2.0 * q[f] + w[f, :, 4:28, :])
        one.append(q[f] + mend(lanes_along(gx[f], q[f]), edge_x[f]) + ty + layers_along(gz[f], q[f]))
    inv, pres = aux(one)
    gy = flux(one, inv, pres, 1)
    start = [0.5 * w[f, :, 8:24, :] for f in range(8)]

    @pl.when(edge)
    def _():
        swap.wait_send()

    for k, c in enumerate((hl_main, hr_main, hl_prev, hr_next, hl_next_in, hr_prev_in, y_prev, y_next)):
        c.wait_send()

    @pl.when(last)
    def _():
        hl_full.wait_send()

    @pl.when(first)
    def _():
        hr_full.wait_send()

    @pl.when(edge)
    def _():
        az_prev.wait_send()
        az_next.wait_send()

    for f in range(8):
        w[f, :, 0:24, :] = one[f]
        fy[f, :, 0:24, :] = gy[f]

    q = [w[f, :, 3:19, :] for f in range(8)]
    inv, pres = aux(q)
    gx = flux(q, inv, pres, 0)
    gz = flux(q, inv, pres, 2)
    tiles = pack(lambda f: q[f], 16)
    for f in range(8):
        def y(k, f=f):
            return fy[f, :, 3 + k:19 + k, :]
        ty = combine([y(1), y(2), y(3)], [y(-1), y(-2), y(-3)])
        ty = ty + VISC * (w[f, :, 4:20, :] - 2.0 * q[f] + w[f, :, 2:18, :])
        out[f] = start[f] + 0.5 * (q[f] + ty + layers_along(gz[f], q[f]))
    inner = [lanes_along(gx[f], q[f]) for f in range(8)]

    @pl.when(edge)
    def _():
        swap.wait_recv()

    got = sq[...]
    near_l = jnp.logical_and(first, cols < 8)
    near_r = jnp.logical_and(last, cols >= 24)
    own_cols = jnp.logical_and(cols >= 8, cols < 24)
    e = []
    for f in range(8):
        ghost = es[16 + f, 0:16, :]
        ghost = jnp.where(near_l, lane_roll(got, 4 * (1 - f)), ghost)
        ghost = jnp.where(near_r, lane_roll(got, 4 * (6 - f)), ghost)
        mid = spread(f, tiles[0], tiles[0], tiles[0], tiles[1], tiles[3], tiles[2], tiles[2], tiles[2])
        e.append(jnp.where(own_cols, mid, ghost))
    inv, pres = aux(e)
    gx = flux(e, inv, pres, 0)
    for f in range(8):
        out[f] = out[f] + 0.5 * mend(inner[f], lanes_along(gx[f], e[f]))


def solution(mesh):
    n_az, n_rad = mesh.shape["az"], mesh.shape["rad"]

    def shards(density, momentum, magnetic, tracer, shear_offset):
        half = n_az // 2 * density.shape[1]
        f32 = jnp.float32
        anywhere = pl.BlockSpec(memory_space=pl.ANY)
        return pl.pallas_call(
            functools.partial(kernel, n_az, n_rad, half),
            out_shape=jax.ShapeDtypeStruct((8, 4, 16, 128), f32),
            in_specs=[pl.BlockSpec(memory_space=pltpu.SMEM)] + [anywhere] * 4,
            out_specs=pl.BlockSpec(memory_space=pltpu.VMEM),
            scratch_shapes=[
                pltpu.VMEM((8, 4, 32, 128), f32),
                pltpu.VMEM((8, 4, 32, 128), f32),
                pltpu.VMEM((4, 32, 128), f32),
                pltpu.VMEM((2, 48, 128), f32),
                pltpu.VMEM((2, 48, 128), f32),
                pltpu.VMEM((64, 128), f32),
                pltpu.VMEM((24, 32, 128), f32),
                pltpu.VMEM((16, 128), f32),
                pltpu.VMEM((16, 128), f32),
                pltpu.SemaphoreType.DMA((4,)),
                pltpu.SemaphoreType.DMA((N_COPY,)),
                pltpu.SemaphoreType.DMA((N_COPY,)),
            ],
            compiler_params=pltpu.CompilerParams(collective_id=0, has_side_effects=True),
        )(shear_offset, density, momentum, magnetic, tracer)

    placed = (
        P(None, "az", "rad"),
        P(None, None, "az", "rad"),
        P(None, None, "az", "rad"),
        P(None, "az", "rad"),
        P(),
    )
    return jax.shard_map(
        shards, mesh=mesh, in_specs=placed, out_specs=P(None, None, "az", "rad"), check_vma=False
    )
```

time: 457 us -> 35.6 us (0.08)
  waiting for transfers between devices: 345 us -> 0 us
  starting transfers between devices: 48.7 us -> 0 us
  local copies, waits for them, and re-layouts: 40.4 us -> 1.67 us
  Pallas kernels: 0 us -> 33.7 us
  between operations: 17.2 us -> 0.01 us
  other arithmetic: 5.71 us -> 0 us
    all_gather x2 -> x0, waiting for transfers between devices: 343 us -> none  [sheared(): collected = lax.all_gather(flat_pair, 'az', axis=0, tiled=True)]
    ppermute x8 -> x0, starting transfers between devices: 48.7 us -> none  [the longest x4 32 us: with_halo(): lax.ppermute(tail, axis, [(i, (i + 1) % count) for i in range(count)])]
    pallas_call x0 -> x1, Pallas kernels: none -> 33.7 us  [shards(): pl.pallas_call(functools.partial(kernel, n_az, n_rad, half), out_shape=ja...]
    reshape x4 -> x0, local copies, waits for them, and re-layouts: 17 us -> none  [the longest x2 16.8 us: sheared(): jnp.transpose(spread, (1, 2, 4, 0, 5, 3))]
    transpose x6 -> x0, local copies, waits for them, and re-layouts: 10.3 us -> none  [the longest x2 10.2 us: sheared(): jnp.transpose(spread, (1, 2, 4, 0, 5, 3))]
    all_gather x2 -> x0, local copies, waits for them, and re-layouts: 4.93 us -> none  [sheared(): collected = lax.all_gather(flat_pair, 'az', axis=0, tiled=True)]
  transfers between devices with their start and end apart: 10 -> 0, of which waited for: 3 -> 0; matrix products, arithmetic and copies ran while one was open for 1% -> 0% of each run, Pallas kernels for 0% -> 0%
where the time goes in v1:
time: 35.6 us; the launch traced here: 35.4 us
  Pallas kernels  33.7 us (95%)
  local copies, waits for them, and re-layouts  1.67 us (5%)
    pallas_call x1, Pallas kernels, shards(): pl.pallas_call(functools.partial(kernel, n_az, n_rad, half), out_shape=ja...  33.7 us
    unnamed x1, local copies, waits for them, and re-layouts  1.67 us

profile of v1, /device:TPU:1, one launch (start us, length us, event | category | flops | bytes accessed | tf_op | source)
XLA Modules:
  0.0 35.4 jit_solution(5212303113541534231)
XLA Ops:
  0.0 33.7 %shard_map.55 = f32[8,4,16,128]{3,2,1,0:T(8,128)} custom-call(s32[2]{0:T(128)} %off_ref.1, f32[4,16,128]{2,1,0:T(8,128)} %den.1, f32[3,4,16,128]{3,2,1,0:T(8,128)} %mom.1, f32[3,4,16,128]{3,2,1,0:T(8,128)} %mag.1, f32[4,16,128]{2,1,0:T(8,128)} %tra.1), custom_call_target="tpu_custom_call" | custom-call | tf_op jit(solution)/shard_map/pallas_call | solution.py:417
  33.7 1.7 %copy.7 = f32[8,4,16,128]{3,2,1,0:T(8,128)} copy(f32[8,4,16,128]{3,2,1,0:T(8,128)} %shard_map.55) | data formatting | bytes 524288

commit v2 on v1

--- a/solution.py
+++ b/solution.py
@@ -74,8 +74,8 @@
     return r + VISC * (lane_roll(u, -32) - 2.0 * u + lane_roll(u, 32))
 
 
-def kernel(n_az, n_rad, half_offset, off_ref, den, mom, mag, tra, out,
-           w, fy, own, bhl, bhr, az, es, sp, sq, in_sem, send, recv):
+def kernel(n_az, n_rad, run, half_offset, off_hbm, den, mom, mag, tra, out,
+           off_ref, w, s1, fy, own, bhl, bhr, az, es, sp, sq, in_sem, send, recv):
     a = lax.axis_index("az")
     r = lax.axis_index("rad")
     first = r == 0
@@ -95,24 +95,33 @@
     def greet(step, to_r):
         pl.semaphore_signal(barrier, inc=1, device_id=dev(step, to_r), device_id_type=MESH)
 
-    for step in (-1, 0, 1):
-        greet(step, r_up)
-        greet(step, r_dn)
+    even = lax.rem(r, 2) == 0
+    odd = jnp.logical_not(even)
+    place = lax.rem(a, run)
+    head, tail = place == 0, place == run - 1
+    odd_head, odd_tail = jnp.logical_and(odd, head), jnp.logical_and(odd, tail)
+
+    @pl.when(even)
+    def _():
+        for step in (-1, 0, 1):
+            greet(step, r_up)
+            greet(step, r_dn)
 
     @pl.when(first)
     def _():
         greet(2, r_dn)
 
-    @pl.when(last)
-    def _():
-        greet(-2, r_up)
-
     @pl.when(edge)
     def _():
         greet(n_az // 2, r)
 
-    greet(1, r)
-    greet(-1, r)
+    @pl.when(jnp.logical_or(even, jnp.logical_not(tail)))
+    def _():
+        greet(1, r)
+
+    @pl.when(jnp.logical_or(even, head))
+    def _():
+        greet(-1, r)
 
     rows = pl.ds(8, 16)
     loads = [
@@ -121,8 +130,10 @@
         pltpu.make_async_copy(mag, w.at[4:7, :, rows], in_sem.at[2]),
         pltpu.make_async_copy(tra, w.at[7, :, rows], in_sem.at[3]),
     ]
+    offsets = pltpu.make_async_copy(off_hbm, off_ref, in_sem.at[4])
     for c in loads:
         c.start()
+    offsets.start()
     w[:, :, 0:2, :] = jnp.ones((8, 4, 2, 128), jnp.float32)
     w[:, :, 30:32, :] = jnp.ones((8, 4, 2, 128), jnp.float32)
     for c in loads:
@@ -156,7 +167,11 @@
         own[t, 8:24, :] = tiles[t]
     az[24:40, :] = jnp.where(first, tiles[0], tiles[2])
 
-    pl.semaphore_wait(barrier, 8 + 2 * edge.astype(jnp.int32))
+    one = jnp.int32(1)
+    zero = jnp.int32(0)
+    along = jnp.where(even, 2 * one, jnp.where(head, zero, jnp.where(tail, 2 * one, one)))
+    across = jnp.where(even, zero, jnp.where(last, 7 * one, 6 * one))
+    pl.semaphore_wait(barrier, along + across + jnp.where(edge, one, zero))
 
     def remote(k, src, dst, step, to_r):
         return pltpu.make_async_remote_copy(
@@ -181,39 +196,96 @@
     y_next = remote(Y_NEXT, w.at[:, :, 8:14], w.at[:, :, 24:30], -1, r)
     swap = remote(SWAP, sp, sq, n_az // 2, r)
 
-    hl_main.start()
-    hr_main.start()
-
-    @pl.when(last)
-    def _():
-        hl_full.start()
-        hl_next_end.start()
-
-    @pl.when(jnp.logical_not(last))
-    def _():
-        hl_next_in.start()
-
-    @pl.when(first)
-    def _():
-        hr_full.start()
-        hr_prev_end.start()
-
-    @pl.when(jnp.logical_not(first))
-    def _():
-        hr_prev_in.start()
-
-    hl_prev.start()
-    hr_next.start()
-
-    @pl.when(edge)
-    def _():
-        az_prev.start()
-        az_next.start()
-
-    y_prev.start()
-    y_next.start()
-
-    zero = jnp.int32(0)
+    def send_strips():
+        hl_main.start()
+        hr_main.start()
+
+        @pl.when(last)
+        def _():
+            hl_full.start()
+            hl_next_end.start()
+
+        @pl.when(jnp.logical_not(last))
+        def _():
+            hl_next_in.start()
+
+        @pl.when(first)
+        def _():
+            hr_full.start()
+            hr_prev_end.start()
+
+        @pl.when(jnp.logical_not(first))
+        def _():
+            hr_prev_in.start()
+
+        hl_prev.start()
+        hr_next.start()
+
+    def send_up():
+        @pl.when(edge)
+        def _():
+            az_prev.start()
+        y_prev.start()
+
+    def send_down():
+        @pl.when(edge)
+        def _():
+            az_next.start()
+        y_next.start()
+
+    pl.when(odd)(send_strips)
+    pl.when(jnp.logical_or(even, tail))(send_up)
+    pl.when(jnp.logical_not(odd_head))(send_down)
+
+    @pl.when(jnp.logical_and(odd, jnp.logical_not(tail)))
+    def _():
+        y_next.wait_recv()
+        send_up()
+
+    @pl.when(odd_head)
+    def _():
+        y_prev.wait_recv()
+        send_down()
+
+    @pl.when(jnp.logical_or(even, tail))
+    def _():
+        y_next.wait_recv()
+
+    @pl.when(jnp.logical_not(odd_head))
+    def _():
+        y_prev.wait_recv()
+
+    cols = lane % 32
+
+    edge_lane = jnp.logical_or(lane < 3, lane >= 125)
+
+    def edges(strip_f):
+        joined = jnp.where(jnp.logical_and(cols >= 5, cols < 8), lane_roll(strip_f, -16), strip_f)
+        return jnp.stack([jnp.where(edge_lane, lane_roll(joined, -(32 * z + 8)), 0.0) for z in range(4)])
+
+    low = pack(lambda f: w[f, :, 0:8, :], 8)
+    high = pack(lambda f: w[f, :, 24:32, :], 8)
+    for t in range(4):
+        own[t, 0:8, :] = low[t]
+        own[t, 24:32, :] = high[t]
+    q = [w[f] for f in range(8)]
+    inv, pres = aux(q)
+    gy = flux(q, inv, pres, 1)
+    for f in range(8):
+        fy[f] = gy[f]
+    q = [w[f, :, 5:29, :] for f in range(8)]
+    inv, pres = aux(q)
+    gx = flux(q, inv, pres, 0)
+    gz = flux(q, inv, pres, 2)
+    for f in range(8):
+        def y(k, f=f):
+            return fy[f, :, 5 + k:29 + k, :]
+        ty = combine([y(1), y(2), y(3)], [y(-1), y(-2), y(-3)])
+        ty = ty + VISC * (w[f, :, 6:30, :] - 2.0 * q[f] + w[f, :, 4:28, :])
+        tx = jnp.where(edge_lane, 0.0, lanes_along(gx[f], q[f]))
+        s1[f, :, 0:24, :] = q[f] + tx + ty + layers_along(gz[f], q[f])
+
+    offsets.wait()
     s_raw = jnp.clip(off_ref[0], 0, 15)
     t_raw = jnp.clip(off_ref[1] - half_offset, 0, 15)
     s_f = jnp.where(first, s_raw, zero)
@@ -257,7 +329,6 @@
     o_r = 21 - t_l - end_l + s_l
     rn2 = jnp.where(last, lead * az[pl.ds(o_r, win), :] + trail * az[pl.ds(o_r + 1, win), :], own[2, 5:29, :])
     e = [spread(f, hlf, hln, ln2, ln2, rn2, rn2, hrn, hrf) for f in range(8)]
-    cols = lane % 32
     in_l = jnp.logical_and(cols >= 8, cols < 16)
     in_r = jnp.logical_and(cols >= 16, cols < 24)
     jump(e, jnp.logical_and(last, in_r), jnp.logical_and(first, in_l))
@@ -297,16 +368,11 @@
     def _():
         swap.start()
 
+    pl.when(even)(send_strips)
+
     for f in range(8):
         es[16 + f, 0:16, :] = strip[f]
 
-    y_prev.wait_recv()
-    y_next.wait_recv()
-    low = pack(lambda f: w[f, :, 0:8, :], 8)
-    high = pack(lambda f: w[f, :, 24:32, :], 8)
-    for t in range(4):
-        own[t, 0:8, :] = low[t]
-        own[t, 24:32, :] = high[t]
     hln0, hln1 = bhl[0, pl.ds(5 + s_f, win), :], bhl[0, pl.ds(5 + s_f + end_f, win), :]
     hln = jnp.where(first, lead * hln0 + trail * hln1, hln0)
     o_r = 21 - s_l
@@ -317,63 +383,15 @@
     jump(e, jnp.logical_and(first, cols < 8), jnp.logical_and(last, cols >= 24))
     inv, pres = aux(e)
     gx = flux(e, inv, pres, 0)
-    edge_x = [lanes_along(gx[f], e[f]) for f in range(8)]
-
-    at_left, at_right = lane < 3, lane >= 125
-
-    def mend(inner, strip_f):
-        fixed = []
-        for z in range(4):
-            from_l = lane_roll(strip_f, -(32 * z + 8))
-            from_r = lane_roll(strip_f, 104 - 32 * z)
-            fixed.append(jnp.where(at_left, from_l, jnp.where(at_right, from_r, inner[z])))
-        return jnp.stack(fixed)
-
-    q = [w[f] for f in range(8)]
+    for f in range(8):
+        s1[f, :, 0:24, :] = s1[f, :, 0:24, :] + edges(lanes_along(gx[f], e[f]))
+
+    q = [s1[f, :, 0:24, :] for f in range(8)]
     inv, pres = aux(q)
     gy = flux(q, inv, pres, 1)
     for f in range(8):
-        fy[f] = gy[f]
-    q = [w[f, :, 5:29, :] for f in range(8)]
-    inv, pres = aux(q)
-    gx = flux(q, inv, pres, 0)
-    gz = flux(q, inv, pres, 2)
-    one = []
-    for f in range(8):
-        def y(k, f=f):
-            return fy[f, :, 5 + k:29 + k, :]
-        ty = combine([y(1), y(2), y(3)], [y(-1), y(-2), y(-3)])
-        ty = ty + VISC * (w[f, :, 6:30, :] - 2.0 * q[f] + w[f, :, 4:28, :])
-        one.append(q[f] + mend(lanes_along(gx[f], q[f]), edge_x[f]) + ty + layers_along(gz[f], q[f]))
-    inv, pres = aux(one)
-    gy = flux(one, inv, pres, 1)
-    start = [0.5 * w[f, :, 8:24, :] for f in range(8)]
-
-    @pl.when(edge)
-    def _():
-        swap.wait_send()
-
-    for k, c in enumerate((hl_main, hr_main, hl_prev, hr_next, hl_next_in, hr_prev_in, y_prev, y_next)):
-        c.wait_send()
-
-    @pl.when(last)
-    def _():
-        hl_full.wait_send()
-
-    @pl.when(first)
-    def _():
-        hr_full.wait_send()
-
-    @pl.when(edge)
-    def _():
-        az_prev.wait_send()
-        az_next.wait_send()
-
-    for f in range(8):
-        w[f, :, 0:24, :] = one[f]
         fy[f, :, 0:24, :] = gy[f]
-
-    q = [w[f, :, 3:19, :] for f in range(8)]
+    q = [s1[f, :, 3:19, :] for f in range(8)]
     inv, pres = aux(q)
     gx = flux(q, inv, pres, 0)
     gz = flux(q, inv, pres, 2)
@@ -382,29 +400,46 @@
         def y(k, f=f):
             return fy[f, :, 3 + k:19 + k, :]
         ty = combine([y(1), y(2), y(3)], [y(-1), y(-2), y(-3)])
-        ty = ty + VISC * (w[f, :, 4:20, :] - 2.0 * q[f] + w[f, :, 2:18, :])
-        out[f] = start[f] + 0.5 * (q[f] + ty + layers_along(gz[f], q[f]))
-    inner = [lanes_along(gx[f], q[f]) for f in range(8)]
+        ty = ty + VISC * (s1[f, :, 4:20, :] - 2.0 * q[f] + s1[f, :, 2:18, :])
+        tx = jnp.where(edge_lane, 0.0, lanes_along(gx[f], q[f]))
+        out[f] = 0.5 * w[f, :, 8:24, :] + 0.5 * (q[f] + tx + ty + layers_along(gz[f], q[f]))
+    own_cols = jnp.logical_and(cols >= 8, cols < 24)
+    for f in range(8):
+        mid = spread(f, tiles[0], tiles[0], tiles[0], tiles[1], tiles[3], tiles[2], tiles[2], tiles[2])
+        es[16 + f, 0:16, :] = jnp.where(own_cols, mid, es[16 + f, 0:16, :])
 
     @pl.when(edge)
     def _():
         swap.wait_recv()
 
     got = sq[...]
-    near_l = jnp.logical_and(first, cols < 8)
-    near_r = jnp.logical_and(last, cols >= 24)
-    own_cols = jnp.logical_and(cols >= 8, cols < 24)
-    e = []
-    for f in range(8):
-        ghost = es[16 + f, 0:16, :]
-        ghost = jnp.where(near_l, lane_roll(got, 4 * (1 - f)), ghost)
-        ghost = jnp.where(near_r, lane_roll(got, 4 * (6 - f)), ghost)
-        mid = spread(f, tiles[0], tiles[0], tiles[0], tiles[1], tiles[3], tiles[2], tiles[2], tiles[2])
-        e.append(jnp.where(own_cols, mid, ghost))
+    got = jnp.where(last, lane_roll(got, 20), got)
+    theirs = jnp.logical_or(jnp.logical_and(first, cols < 8), jnp.logical_and(last, cols >= 24))
+    e = [jnp.where(theirs, lane_roll(got, 4 * (1 - f)), es[16 + f, 0:16, :]) for f in range(8)]
     inv, pres = aux(e)
     gx = flux(e, inv, pres, 0)
     for f in range(8):
-        out[f] = out[f] + 0.5 * mend(inner[f], lanes_along(gx[f], e[f]))
+        out[f] = out[f] + edges(0.5 * lanes_along(gx[f], e[f]))
+
+    @pl.when(edge)
+    def _():
+        swap.wait_send()
+
+    for c in (hl_main, hr_main, hl_prev, hr_next, hl_next_in, hr_prev_in, y_prev, y_next):
+        c.wait_send()
+
+    @pl.when(last)
+    def _():
+        hl_full.wait_send()
+
+    @pl.when(first)
+    def _():
+        hr_full.wait_send()
+
+    @pl.when(edge)
+    def _():
+        az_prev.wait_send()
+        az_next.wait_send()
 
 
 def solution(mesh):
@@ -415,11 +450,13 @@
         f32 = jnp.float32
         anywhere = pl.BlockSpec(memory_space=pl.ANY)
         return pl.pallas_call(
-            functools.partial(kernel, n_az, n_rad, half),
-            out_shape=jax.ShapeDtypeStruct((8, 4, 16, 128), f32),
-            in_specs=[pl.BlockSpec(memory_space=pltpu.SMEM)] + [anywhere] * 4,
+            functools.partial(kernel, n_az, n_rad, 12 if n_az % 12 == 0 else 2, half),
+            out_shape=pltpu.VMEM((8, 4, 16, 128), f32),
+            in_specs=[anywhere] * 5,
             out_specs=pl.BlockSpec(memory_space=pltpu.VMEM),
             scratch_shapes=[
+                pltpu.SMEM((2,), jnp.int32),
+                pltpu.VMEM((8, 4, 32, 128), f32),
                 pltpu.VMEM((8, 4, 32, 128), f32),
                 pltpu.VMEM((8, 4, 32, 128), f32),
                 pltpu.VMEM((4, 32, 128), f32),
@@ -429,7 +466,7 @@
                 pltpu.VMEM((24, 32, 128), f32),
                 pltpu.VMEM((16, 128), f32),
                 pltpu.VMEM((16, 128), f32),
-                pltpu.SemaphoreType.DMA((4,)),
+                pltpu.SemaphoreType.DMA((5,)),
                 pltpu.SemaphoreType.DMA((N_COPY,)),
                 pltpu.SemaphoreType.DMA((N_COPY,)),
             ],

time: 35.6 us -> 29.6 us (0.83)
  Pallas kernels: 33.7 us -> 28.8 us
  local copies, waits for them, and re-layouts: 1.67 us -> 0.71 us
    pallas_call x1, Pallas kernels: 33.7 us -> 28.8 us  [shards(): pl.pallas_call(functools.partial(kernel, n_az, n_rad, 12 if n_az % 12 ==...]
    unnamed x1, local copies, waits for them, and re-layouts: 1.67 us -> 0.71 us
where the time goes in v2:
time: 29.6 us; the launch traced here: 29.5 us
  Pallas kernels  28.8 us (97%)
  local copies, waits for them, and re-layouts  0.71 us (2%)
    pallas_call x1, Pallas kernels, shards(): pl.pallas_call(functools.partial(kernel, n_az, n_rad, 12 if n_az % 12 ==...  28.8 us
    unnamed x1, local copies, waits for them, and re-layouts  0.71 us

profile of v2, /device:TPU:1, one launch (start us, length us, event | category | flops | bytes accessed | tf_op | source)
XLA Modules:
  0.0 29.5 jit_solution(6335733540266303836)
XLA Ops:
  0.0 28.8 %shard_map.55 = f32[8,4,16,128]{3,2,1,0:T(8,128)S(1)} custom-call(s32[2]{0:T(128)} %off_hbm.1, f32[4,16,128]{2,1,0:T(8,128)} %den.1, f32[3,4,16,128]{3,2,1,0:T(8,128)} %mom.1, f32[3,4,16,128]{3,2,1,0:T(8,128)} %mag.1, f32[4,16,128]{2,1,0:T(8,128)} %tra.1), custom_call_target="tpu_custom_call" | custom-call | tf_op jit(solution)/shard_map/pallas_call | solution.py:452
  28.8 0.7 %copy.7 = f32[8,4,16,128]{3,2,1,0:T(8,128)} copy(f32[8,4,16,128]{3,2,1,0:T(8,128)S(1)} %shard_map.55) | data formatting | bytes 524288

commit v3 on v2

--- a/solution.py
+++ b/solution.py
@@ -21,8 +21,8 @@
 lead = 1.0 - frac_weight
 trail = frac_weight
 
-Y_PREV, Y_NEXT, HL_MAIN, HL_PREV, HL_NEXT, HL_FULL, HR_MAIN, HR_NEXT, HR_PREV, HR_FULL, AZ_PREV, AZ_NEXT, SWAP = range(13)
-N_COPY = 13
+S_MAIN, S_CORNER, S_FULL, S_AZ, S_Y, S_SWAP = range(6)
+R_LEFT, R_RIGHT, R_FULL, R_AZ, R_PREV, R_NEXT, R_SWAP = range(7)
 
 
 def flux(q, inv, pres, d):
@@ -75,7 +75,7 @@
 
 
 def kernel(n_az, n_rad, run, half_offset, off_hbm, den, mom, mag, tra, out,
-           off_ref, w, s1, fy, own, bhl, bhr, az, es, sp, sq, in_sem, send, recv):
+           off_ref, w, s1, fy, own, bhl, bhr, az, es, sp, sq, in_sem, send, recv, go):
     a = lax.axis_index("az")
     r = lax.axis_index("rad")
     first = r == 0
@@ -90,6 +90,18 @@
     def dev(step, to_r):
         return (at(step), to_r)
 
+    rows = pl.ds(8, 16)
+    loads = [
+        pltpu.make_async_copy(den, w.at[0, :, rows], in_sem.at[0]),
+        pltpu.make_async_copy(mom, w.at[1:4, :, rows], in_sem.at[0]),
+        pltpu.make_async_copy(mag, w.at[4:7, :, rows], in_sem.at[0]),
+        pltpu.make_async_copy(tra, w.at[7, :, rows], in_sem.at[0]),
+    ]
+    offsets = pltpu.make_async_copy(off_hbm, off_ref, in_sem.at[1])
+    for c in loads:
+        c.start()
+    offsets.start()
+
     barrier = pltpu.get_barrier_semaphore()
 
     def greet(step, to_r):
@@ -111,7 +123,10 @@
     def _():
         greet(2, r_dn)
 
-    @pl.when(edge)
+    greets_half = jnp.logical_or(first, jnp.logical_and(last, head))
+    told = jnp.logical_and(last, jnp.logical_not(head))
+
+    @pl.when(greets_half)
     def _():
         greet(n_az // 2, r)
 
@@ -123,21 +138,10 @@
     def _():
         greet(-1, r)
 
-    rows = pl.ds(8, 16)
-    loads = [
-        pltpu.make_async_copy(den, w.at[0, :, rows], in_sem.at[0]),
-        pltpu.make_async_copy(mom, w.at[1:4, :, rows], in_sem.at[1]),
-        pltpu.make_async_copy(mag, w.at[4:7, :, rows], in_sem.at[2]),
-        pltpu.make_async_copy(tra, w.at[7, :, rows], in_sem.at[3]),
-    ]
-    offsets = pltpu.make_async_copy(off_hbm, off_ref, in_sem.at[4])
-    for c in loads:
-        c.start()
-    offsets.start()
     w[:, :, 0:2, :] = jnp.ones((8, 4, 2, 128), jnp.float32)
     w[:, :, 30:32, :] = jnp.ones((8, 4, 2, 128), jnp.float32)
-    for c in loads:
-        c.wait()
+    block = w.at[:, :, rows]
+    pltpu.make_async_copy(block, block, in_sem.at[0]).wait()
 
     lane = lax.broadcasted_iota(jnp.int32, (1, 128), 1)
     group = lane // 4
@@ -171,34 +175,36 @@
     zero = jnp.int32(0)
     along = jnp.where(even, 2 * one, jnp.where(head, zero, jnp.where(tail, 2 * one, one)))
     across = jnp.where(even, zero, jnp.where(last, 7 * one, 6 * one))
-    pl.semaphore_wait(barrier, along + across + jnp.where(edge, one, zero))
-
-    def remote(k, src, dst, step, to_r):
+    pl.semaphore_wait(barrier, along + across + jnp.where(greets_half, one, zero))
+
+    def remote(k, n, src, dst, step, to_r):
         return pltpu.make_async_remote_copy(
-            src_ref=src, dst_ref=dst, send_sem=send.at[k], recv_sem=recv.at[k],
+            src_ref=src, dst_ref=dst, send_sem=send.at[k], recv_sem=recv.at[n],
             device_id=dev(step, to_r), device_id_type=MESH)
+
+    def arrived(ref, sem):
+        pltpu.make_async_copy(ref, ref, sem).wait()
 
     own_l, own_r = own.at[0:2, 8:24], own.at[2:4, 8:24]
     ln, rn = own.at[0], own.at[2]
-    hl_main = remote(HL_MAIN, own_r, bhl.at[:, 8:24], 0, r_up)
-    hr_main = remote(HR_MAIN, own_l, bhr.at[:, 24:40], 0, r_dn)
-    hl_full = remote(HL_FULL, own_r, bhl.at[:, 24:40], -1, r_up)
-    hr_full = remote(HR_FULL, own_l, bhr.at[:, 8:24], 1, r_dn)
-    hl_prev = remote(HL_PREV, rn.at[21:24], bhl.at[0, 5:8], 1, r_up)
-    hr_next = remote(HR_NEXT, ln.at[8:11], bhr.at[0, 40:43], -1, r_dn)
-    hl_next_in = remote(HL_NEXT, rn.at[8:11], bhl.at[0, 24:27], -1, r_up)
-    hl_next_end = remote(HL_NEXT, rn.at[8:11], bhl.at[0, 40:43], -2, r_up)
-    hr_prev_in = remote(HR_PREV, ln.at[21:24], bhr.at[0, 21:24], 1, r_dn)
-    hr_prev_end = remote(HR_PREV, ln.at[21:24], bhr.at[0, 5:8], 2, r_dn)
-    az_prev = remote(AZ_PREV, az.at[24:40], az.at[8:24], 1, r)
-    az_next = remote(AZ_NEXT, az.at[24:40], az.at[40:56], -1, r)
-    y_prev = remote(Y_PREV, w.at[:, :, 18:24], w.at[:, :, 2:8], 1, r)
-    y_next = remote(Y_NEXT, w.at[:, :, 8:14], w.at[:, :, 24:30], -1, r)
-    swap = remote(SWAP, sp, sq, n_az // 2, r)
-
-    def send_strips():
+    hl_main = remote(S_MAIN, R_LEFT, own_r, bhl.at[:, 8:24], 0, r_up)
+    hr_main = remote(S_MAIN, R_RIGHT, own_l, bhr.at[:, 24:40], 0, r_dn)
+    hl_full = remote(S_FULL, R_FULL, own_r, bhl.at[:, 24:40], -1, r_up)
+    hr_full = remote(S_FULL, R_FULL, own_l, bhr.at[:, 8:24], 1, r_dn)
+    hl_prev = remote(S_CORNER, R_LEFT, rn.at[21:24], bhl.at[0, 5:8], 1, r_up)
+    hr_next = remote(S_CORNER, R_RIGHT, ln.at[8:11], bhr.at[0, 40:43], -1, r_dn)
+    hl_next_in = remote(S_CORNER, R_LEFT, rn.at[8:11], bhl.at[0, 24:27], -1, r_up)
+    hl_next_end = remote(S_CORNER, R_LEFT, rn.at[8:11], bhl.at[0, 40:43], -2, r_up)
+    hr_prev_in = remote(S_CORNER, R_RIGHT, ln.at[21:24], bhr.at[0, 21:24], 1, r_dn)
+    hr_prev_end = remote(S_CORNER, R_RIGHT, ln.at[21:24], bhr.at[0, 5:8], 2, r_dn)
+    az_prev = remote(S_AZ, R_AZ, az.at[24:40], az.at[8:24], 1, r)
+    az_next = remote(S_AZ, R_AZ, az.at[24:40], az.at[40:56], -1, r)
+    y_prev = remote(S_Y, R_PREV, w.at[:, :, 18:24], w.at[:, :, 2:8], 1, r)
+    y_next = remote(S_Y, R_NEXT, w.at[:, :, 8:14], w.at[:, :, 24:30], -1, r)
+    swap = remote(S_SWAP, R_SWAP, sp, sq, n_az // 2, r)
+
+    def send_right():
         hl_main.start()
-        hr_main.start()
 
         @pl.when(last)
         def _():
@@ -209,6 +215,11 @@
         def _():
             hl_next_in.start()
 
+        hl_prev.start()
+
+    def send_left():
+        hr_main.start()
+
         @pl.when(first)
         def _():
             hr_full.start()
@@ -218,7 +229,6 @@
         def _():
             hr_prev_in.start()
 
-        hl_prev.start()
         hr_next.start()
 
     def send_up():
@@ -233,7 +243,8 @@
             az_next.start()
         y_next.start()
 
-    pl.when(odd)(send_strips)
+    pl.when(odd)(send_right)
+    pl.when(odd)(send_left)
     pl.when(jnp.logical_or(even, tail))(send_up)
     pl.when(jnp.logical_not(odd_head))(send_down)
 
@@ -295,25 +306,18 @@
     end_l = jnp.where(last, 1, zero)
     end_f = jnp.where(first, 1, zero)
 
-    hl_main.wait_recv()
-    hr_main.wait_recv()
-    hl_prev.wait_recv()
-    hr_next.wait_recv()
-    hl_next_in.wait_recv()
-    hr_prev_in.wait_recv()
-
-    @pl.when(first)
-    def _():
-        hl_full.wait_recv()
-
-    @pl.when(last)
-    def _():
-        hr_full.wait_recv()
+    arrived(az.at[0:38], recv.at[R_RIGHT])
+    pl.when(last)(hr_full.wait_recv)
+
+    pl.when(even)(send_right)
+    arrived(az.at[0:38], recv.at[R_LEFT])
+    pl.when(first)(hl_full.wait_recv)
+
+    pl.when(even)(send_left)
 
     @pl.when(edge)
     def _():
-        az_prev.wait_recv()
-        az_next.wait_recv()
+        arrived(az.at[0:32], recv.at[R_AZ])
 
     def jump(fields, mask_l, mask_r):
         add = jnp.where(mask_l, shear_speed, 0.0) - jnp.where(mask_r, shear_speed, 0.0)
@@ -364,11 +368,13 @@
         packed = jnp.where(slot_is[f], lane_roll(src, 4 * (f - 1)), packed)
     sp[...] = packed
 
+    @pl.when(told)
+    def _():
+        pl.semaphore_wait(go, 1)
+
     @pl.when(edge)
     def _():
         swap.start()
-
-    pl.when(even)(send_strips)
 
     for f in range(8):
         es[16 + f, 0:16, :] = strip[f]
@@ -408,9 +414,19 @@
         mid = spread(f, tiles[0], tiles[0], tiles[0], tiles[1], tiles[3], tiles[2], tiles[2], tiles[2])
         es[16 + f, 0:16, :] = jnp.where(own_cols, mid, es[16 + f, 0:16, :])
 
+    arrived(own.at[:, 8:24], send.at[S_MAIN])
+    arrived(az.at[0:12], send.at[S_CORNER])
+    arrived(w.at[:, :, 0:12], send.at[S_Y])
+
     @pl.when(edge)
     def _():
+        arrived(own.at[0:2, 8:24], send.at[S_FULL])
+        arrived(az.at[0:32], send.at[S_AZ])
         swap.wait_recv()
+
+    @pl.when(jnp.logical_and(first, jnp.logical_not(head)))
+    def _():
+        pl.semaphore_signal(go, inc=1, device_id=(a, r_dn), device_id_type=MESH)
 
     got = sq[...]
     got = jnp.where(last, lane_roll(got, 20), got)
@@ -421,25 +437,7 @@
     for f in range(8):
         out[f] = out[f] + edges(0.5 * lanes_along(gx[f], e[f]))
 
-    @pl.when(edge)
-    def _():
-        swap.wait_send()
-
-    for c in (hl_main, hr_main, hl_prev, hr_next, hl_next_in, hr_prev_in, y_prev, y_next):
-        c.wait_send()
-
-    @pl.when(last)
-    def _():
-        hl_full.wait_send()
-
-    @pl.when(first)
-    def _():
-        hr_full.wait_send()
-
-    @pl.when(edge)
-    def _():
-        az_prev.wait_send()
-        az_next.wait_send()
+    pl.when(edge)(swap.wait_send)
 
 
 def solution(mesh):
@@ -466,9 +464,10 @@
                 pltpu.VMEM((24, 32, 128), f32),
                 pltpu.VMEM((16, 128), f32),
                 pltpu.VMEM((16, 128), f32),
-                pltpu.SemaphoreType.DMA((5,)),
-                pltpu.SemaphoreType.DMA((N_COPY,)),
-                pltpu.SemaphoreType.DMA((N_COPY,)),
+                pltpu.SemaphoreType.DMA((2,)),
+                pltpu.SemaphoreType.DMA((6,)),
+                pltpu.SemaphoreType.DMA((7,)),
+                pltpu.SemaphoreType.REGULAR,
             ],
             compiler_params=pltpu.CompilerParams(collective_id=0, has_side_effects=True),
         )(shear_offset, density, momentum, magnetic, tracer)

time: 29.6 us -> 29.4 us (level)
  Pallas kernels: 28.8 us -> 28.5 us
where the time goes in v3:
time: 29.4 us; the launch traced here: 29.2 us
  Pallas kernels  28.5 us (97%)
  local copies, waits for them, and re-layouts  0.71 us (2%)
    pallas_call x1, Pallas kernels, shards(): pl.pallas_call(functools.partial(kernel, n_az, n_rad, 12 if n_az % 12 ==...  28.5 us
    unnamed x1, local copies, waits for them, and re-layouts  0.71 us

profile of v3, /device:TPU:1, one launch (start us, length us, event | category | flops | bytes accessed | tf_op | source)
XLA Modules:
  0.0 29.2 jit_solution(2132159691759650113)
XLA Ops:
  0.0 28.5 %shard_map.55 = f32[8,4,16,128]{3,2,1,0:T(8,128)S(1)} custom-call(s32[2]{0:T(128)} %off_hbm.1, f32[4,16,128]{2,1,0:T(8,128)} %den.1, f32[3,4,16,128]{3,2,1,0:T(8,128)} %mom.1, f32[3,4,16,128]{3,2,1,0:T(8,128)} %mag.1, f32[4,16,128]{2,1,0:T(8,128)} %tra.1), custom_call_target="tpu_custom_call" | custom-call | tf_op jit(solution)/shard_map/pallas_call | solution.py:450
  28.5 0.7 %copy.7 = f32[8,4,16,128]{3,2,1,0:T(8,128)} copy(f32[8,4,16,128]{3,2,1,0:T(8,128)S(1)} %shard_map.55) | data formatting | bytes 524288

commit v4 on v3

--- a/solution.py
+++ b/solution.py
@@ -75,7 +75,7 @@
 
 
 def kernel(n_az, n_rad, run, half_offset, off_hbm, den, mom, mag, tra, out,
-           off_ref, w, s1, fy, own, bhl, bhr, az, es, sp, sq, in_sem, send, recv, go):
+           off_ref, w, s1, fy, own, far, far_l, far_r, bhl, bhr, az, es, sp, sq, in_sem, send, recv, go):
     a = lax.axis_index("az")
     r = lax.axis_index("rad")
     first = r == 0
@@ -91,12 +91,11 @@
         return (at(step), to_r)
 
     rows = pl.ds(8, 16)
-    loads = [
-        pltpu.make_async_copy(den, w.at[0, :, rows], in_sem.at[0]),
-        pltpu.make_async_copy(mom, w.at[1:4, :, rows], in_sem.at[0]),
-        pltpu.make_async_copy(mag, w.at[4:7, :, rows], in_sem.at[0]),
-        pltpu.make_async_copy(tra, w.at[7, :, rows], in_sem.at[0]),
-    ]
+    loads = [pltpu.make_async_copy(den, w.at[0, :, rows], in_sem.at[0])]
+    for i in range(3):
+        loads.append(pltpu.make_async_copy(mom.at[i], w.at[1 + i, :, rows], in_sem.at[0]))
+        loads.append(pltpu.make_async_copy(mag.at[i], w.at[4 + i, :, rows], in_sem.at[0]))
+    loads.append(pltpu.make_async_copy(tra, w.at[7, :, rows], in_sem.at[0]))
     offsets = pltpu.make_async_copy(off_hbm, off_ref, in_sem.at[1])
     for c in loads:
         c.start()
@@ -169,6 +168,9 @@
     tiles = pack(lambda f: w[f, :, 8:24, :], 16)
     for t in range(4):
         own[t, 8:24, :] = tiles[t]
+    inner_two = lane % 4 < 2
+    far[0] = jnp.where(inner_two, tiles[1][0:8], lane_roll(tiles[1][8:16], 2))
+    far[1] = jnp.where(inner_two, lane_roll(tiles[3][8:16], -2), tiles[3][0:8])
     az[24:40, :] = jnp.where(first, tiles[0], tiles[2])
 
     one = jnp.int32(1)
@@ -185,12 +187,16 @@
     def arrived(ref, sem):
         pltpu.make_async_copy(ref, ref, sem).wait()
 
-    own_l, own_r = own.at[0:2, 8:24], own.at[2:4, 8:24]
+    own_l, own_r = own.at[0, 8:24], own.at[2, 8:24]
     ln, rn = own.at[0], own.at[2]
-    hl_main = remote(S_MAIN, R_LEFT, own_r, bhl.at[:, 8:24], 0, r_up)
-    hr_main = remote(S_MAIN, R_RIGHT, own_l, bhr.at[:, 24:40], 0, r_dn)
-    hl_full = remote(S_FULL, R_FULL, own_r, bhl.at[:, 24:40], -1, r_up)
-    hr_full = remote(S_FULL, R_FULL, own_l, bhr.at[:, 8:24], 1, r_dn)
+    hl_main = (remote(S_MAIN, R_LEFT, own_r, bhl.at[0, 8:24], 0, r_up),
+               remote(S_MAIN, R_LEFT, far.at[1], far_l.at[0], 0, r_up))
+    hr_main = (remote(S_MAIN, R_RIGHT, own_l, bhr.at[0, 24:40], 0, r_dn),
+               remote(S_MAIN, R_RIGHT, far.at[0], far_r.at[0], 0, r_dn))
+    hl_full = (remote(S_FULL, R_FULL, own_r, bhl.at[0, 24:40], -1, r_up),
+               remote(S_FULL, R_FULL, far.at[1], far_l.at[1], -1, r_up))
+    hr_full = (remote(S_FULL, R_FULL, own_l, bhr.at[0, 8:24], 1, r_dn),
+               remote(S_FULL, R_FULL, far.at[0], far_r.at[1], 1, r_dn))
     hl_prev = remote(S_CORNER, R_LEFT, rn.at[21:24], bhl.at[0, 5:8], 1, r_up)
     hr_next = remote(S_CORNER, R_RIGHT, ln.at[8:11], bhr.at[0, 40:43], -1, r_dn)
     hl_next_in = remote(S_CORNER, R_LEFT, rn.at[8:11], bhl.at[0, 24:27], -1, r_up)
@@ -204,11 +210,13 @@
     swap = remote(S_SWAP, R_SWAP, sp, sq, n_az // 2, r)
 
     def send_right():
-        hl_main.start()
+        for c in hl_main:
+            c.start()
 
         @pl.when(last)
         def _():
-            hl_full.start()
+            for c in hl_full:
+                c.start()
             hl_next_end.start()
 
         @pl.when(jnp.logical_not(last))
@@ -218,11 +226,13 @@
         hl_prev.start()
 
     def send_left():
-        hr_main.start()
+        for c in hr_main:
+            c.start()
 
         @pl.when(first)
         def _():
-            hr_full.start()
+            for c in hr_full:
+                c.start()
             hr_prev_end.start()
 
         @pl.when(jnp.logical_not(first))
@@ -243,8 +253,12 @@
             az_next.start()
         y_next.start()
 
-    pl.when(odd)(send_right)
-    pl.when(odd)(send_left)
+    @pl.when(odd)
+    def _():
+        send_right()
+        send_left()
+        arrived(az.at[0:48], send.at[S_MAIN])
+
     pl.when(jnp.logical_or(even, tail))(send_up)
     pl.when(jnp.logical_not(odd_head))(send_down)
 
@@ -306,12 +320,18 @@
     end_l = jnp.where(last, 1, zero)
     end_f = jnp.where(first, 1, zero)
 
-    arrived(az.at[0:38], recv.at[R_RIGHT])
-    pl.when(last)(hr_full.wait_recv)
+    arrived(az.at[0:30], recv.at[R_RIGHT])
+
+    @pl.when(last)
+    def _():
+        arrived(az.at[0:24], recv.at[R_FULL])
 
     pl.when(even)(send_right)
-    arrived(az.at[0:38], recv.at[R_LEFT])
-    pl.when(first)(hl_full.wait_recv)
+    arrived(az.at[0:30], recv.at[R_LEFT])
+
+    @pl.when(first)
+    def _():
+        arrived(az.at[0:24], recv.at[R_FULL])
 
     pl.when(even)(send_left)
 
@@ -324,6 +344,11 @@
         fields[2] = jnp.where(jnp.logical_or(mask_l, mask_r), fields[2] + add * fields[0], fields[2])
 
     win = 24
+    for k, row in ((0, 8), (1, 24)):
+        bhl[1, row:row + 8, :] = far_l[k]
+        bhl[1, row + 8:row + 16, :] = lane_roll(far_l[k], 2)
+        bhr[1, 32 - row:40 - row, :] = far_r[k]
+        bhr[1, 40 - row:48 - row, :] = lane_roll(far_r[k], -2)
     hlf = bhl[1, pl.ds(5 + t_f, win), :]
     hln = bhl[0, pl.ds(5 + t_f, win), :]
     hrf = bhr[1, pl.ds(21 - t_l - end_l, win), :]
@@ -414,13 +439,16 @@
         mid = spread(f, tiles[0], tiles[0], tiles[0], tiles[1], tiles[3], tiles[2], tiles[2], tiles[2])
         es[16 + f, 0:16, :] = jnp.where(own_cols, mid, es[16 + f, 0:16, :])
 
-    arrived(own.at[:, 8:24], send.at[S_MAIN])
+    @pl.when(even)
+    def _():
+        arrived(az.at[0:48], send.at[S_MAIN])
+
     arrived(az.at[0:12], send.at[S_CORNER])
     arrived(w.at[:, :, 0:12], send.at[S_Y])
 
     @pl.when(edge)
     def _():
-        arrived(own.at[0:2, 8:24], send.at[S_FULL])
+        arrived(az.at[0:24], send.at[S_FULL])
         arrived(az.at[0:32], send.at[S_AZ])
         swap.wait_recv()
 
@@ -458,6 +486,9 @@
                 pltpu.VMEM((8, 4, 32, 128), f32),
                 pltpu.VMEM((8, 4, 32, 128), f32),
                 pltpu.VMEM((4, 32, 128), f32),
+                pltpu.VMEM((2, 8, 128), f32),
+                pltpu.VMEM((2, 8, 128), f32),
+                pltpu.VMEM((2, 8, 128), f32),
                 pltpu.VMEM((2, 48, 128), f32),
                 pltpu.VMEM((2, 48, 128), f32),
                 pltpu.VMEM((64, 128), f32),

time: 29.4 us -> 29.2 us (level)
  no operation moved by 1% of the time
where the time goes in v4:
time: 29.2 us; the launch traced here: 29 us
  Pallas kernels  28.3 us (97%)
  local copies, waits for them, and re-layouts  0.71 us (2%)
    pallas_call x1, Pallas kernels, shards(): pl.pallas_call(functools.partial(kernel, n_az, n_rad, 12 if n_az % 12 ==...  28.3 us
    unnamed x1, local copies, waits for them, and re-layouts  0.71 us

profile of v4, /device:TPU:1, one launch (start us, length us, event | category | flops | bytes accessed | tf_op | source)
XLA Modules:
  0.0 29.0 jit_solution(11512635999525019305)
XLA Ops:
  0.0 28.3 %shard_map.55 = f32[8,4,16,128]{3,2,1,0:T(8,128)S(1)} custom-call(s32[2]{0:T(128)} %off_hbm.1, f32[4,16,128]{2,1,0:T(8,128)} %den.1, f32[3,4,16,128]{3,2,1,0:T(8,128)} %mom.1, f32[3,4,16,128]{3,2,1,0:T(8,128)} %mag.1, f32[4,16,128]{2,1,0:T(8,128)} %tra.1), custom_call_target="tpu_custom_call" | custom-call | tf_op jit(solution)/shard_map/pallas_call | solution.py:478
  28.3 0.7 %copy.7 = f32[8,4,16,128]{3,2,1,0:T(8,128)} copy(f32[8,4,16,128]{3,2,1,0:T(8,128)S(1)} %shard_map.55) | data formatting | bytes 524288

commit v5 on v4

--- a/solution.py
+++ b/solution.py
@@ -333,7 +333,6 @@
     def _():
         arrived(az.at[0:24], recv.at[R_FULL])
 
-    pl.when(even)(send_left)
 
     @pl.when(edge)
     def _():
@@ -400,6 +399,8 @@
     @pl.when(edge)
     def _():
         swap.start()
+
+    pl.when(even)(send_left)
 
     for f in range(8):
         es[16 + f, 0:16, :] = strip[f]

time: 29.2 us -> 29.2 us (level)
  no operation moved by 1% of the time
where the time goes in v5:
time: 29.2 us; the launch traced here: 29 us
  Pallas kernels  28.3 us (97%)
  local copies, waits for them, and re-layouts  0.71 us (2%)
    pallas_call x1, Pallas kernels, shards(): pl.pallas_call(functools.partial(kernel, n_az, n_rad, 12 if n_az % 12 ==...  28.3 us
    unnamed x1, local copies, waits for them, and re-layouts  0.71 us

profile of v5, /device:TPU:1, one launch (start us, length us, event | category | flops | bytes accessed | tf_op | source)
XLA Modules:
  0.0 29.0 jit_solution(6706467715427364263)
XLA Ops:
  0.0 28.3 %shard_map.55 = f32[8,4,16,128]{3,2,1,0:T(8,128)S(1)} custom-call(s32[2]{0:T(128)} %off_hbm.1, f32[4,16,128]{2,1,0:T(8,128)} %den.1, f32[3,4,16,128]{3,2,1,0:T(8,128)} %mom.1, f32[3,4,16,128]{3,2,1,0:T(8,128)} %mag.1, f32[4,16,128]{2,1,0:T(8,128)} %tra.1), custom_call_target="tpu_custom_call" | custom-call | tf_op jit(solution)/shard_map/pallas_call | solution.py:479
  28.3 0.7 %copy.7 = f32[8,4,16,128]{3,2,1,0:T(8,128)} copy(f32[8,4,16,128]{3,2,1,0:T(8,128)S(1)} %shard_map.55) | data formatting | bytes 524288

commit v6 on v4

--- a/solution.py
+++ b/solution.py
@@ -74,7 +74,28 @@
     return r + VISC * (lane_roll(u, -32) - 2.0 * u + lane_roll(u, 32))
 
 
-def kernel(n_az, n_rad, run, half_offset, off_hbm, den, mom, mag, tra, out,
+def edge_lanes(lane):
+    return jnp.logical_or(lane < 3, lane >= 125)
+
+
+def edges(strip_f, lane):
+    cols = lane % 32
+    joined = jnp.where(jnp.logical_and(cols >= 5, cols < 8), lane_roll(strip_f, -16), strip_f)
+    return jnp.stack([jnp.where(edge_lanes(lane), lane_roll(joined, -(32 * z + 8)), 0.0) for z in range(4)])
+
+
+def finish(pre, part, result, buf, sem):
+    lane = lax.broadcasted_iota(jnp.int32, (1, 128), 1)
+    copies = [pltpu.make_async_copy(buf.at[f], result.at[f], sem) for f in range(8)]
+    for f in range(8):
+        buf[f] = pre[f] + edges(part[f], lane)
+        if f:
+            copies[f - 1].start()
+    copies[7].start()
+    pltpu.make_async_copy(buf, result, sem).wait()
+
+
+def kernel(n_az, n_rad, run, half_offset, off_hbm, den, mom, mag, tra, out, part,
            off_ref, w, s1, fy, own, far, far_l, far_r, bhl, bhr, az, es, sp, sq, in_sem, send, recv, go):
     a = lax.axis_index("az")
     r = lax.axis_index("rad")
@@ -282,11 +303,7 @@
 
     cols = lane % 32
 
-    edge_lane = jnp.logical_or(lane < 3, lane >= 125)
-
-    def edges(strip_f):
-        joined = jnp.where(jnp.logical_and(cols >= 5, cols < 8), lane_roll(strip_f, -16), strip_f)
-        return jnp.stack([jnp.where(edge_lane, lane_roll(joined, -(32 * z + 8)), 0.0) for z in range(4)])
+    edge_lane = edge_lanes(lane)
 
     low = pack(lambda f: w[f, :, 0:8, :], 8)
     high = pack(lambda f: w[f, :, 24:32, :], 8)
@@ -415,7 +432,7 @@
     inv, pres = aux(e)
     gx = flux(e, inv, pres, 0)
     for f in range(8):
-        s1[f, :, 0:24, :] = s1[f, :, 0:24, :] + edges(lanes_along(gx[f], e[f]))
+        s1[f, :, 0:24, :] = s1[f, :, 0:24, :] + edges(lanes_along(gx[f], e[f]), lane)
 
     q = [s1[f, :, 0:24, :] for f in range(8)]
     inv, pres = aux(q)
@@ -463,7 +480,7 @@
     inv, pres = aux(e)
     gx = flux(e, inv, pres, 0)
     for f in range(8):
-        out[f] = out[f] + edges(0.5 * lanes_along(gx[f], e[f]))
+        part[f] = 0.5 * lanes_along(gx[f], e[f])
 
     pl.when(edge)(swap.wait_send)
 
@@ -475,11 +492,12 @@
         half = n_az // 2 * density.shape[1]
         f32 = jnp.float32
         anywhere = pl.BlockSpec(memory_space=pl.ANY)
-        return pl.pallas_call(
+        vmem = pl.BlockSpec(memory_space=pltpu.VMEM)
+        pre, part = pl.pallas_call(
             functools.partial(kernel, n_az, n_rad, 12 if n_az % 12 == 0 else 2, half),
-            out_shape=pltpu.VMEM((8, 4, 16, 128), f32),
+            out_shape=(pltpu.VMEM((8, 4, 16, 128), f32), pltpu.VMEM((8, 16, 128), f32)),
             in_specs=[anywhere] * 5,
-            out_specs=pl.BlockSpec(memory_space=pltpu.VMEM),
+            out_specs=(vmem, vmem),
             scratch_shapes=[
                 pltpu.SMEM((2,), jnp.int32),
                 pltpu.VMEM((8, 4, 32, 128), f32),
@@ -502,6 +520,13 @@
             ],
             compiler_params=pltpu.CompilerParams(collective_id=0, has_side_effects=True),
         )(shear_offset, density, momentum, magnetic, tracer)
+        return pl.pallas_call(
+            finish,
+            out_shape=jax.ShapeDtypeStruct((8, 4, 16, 128), f32),
+            in_specs=[vmem, vmem],
+            out_specs=anywhere,
+            scratch_shapes=[pltpu.VMEM((8, 4, 16, 128), f32), pltpu.SemaphoreType.DMA],
+        )(*[pltpu.with_memory_space_constraint(q, pltpu.VMEM) for q in (pre, part)])
 
     placed = (
         P(None, "az", "rad"),

time: 29.2 us -> 29.2 us (level)
  local copies, waits for them, and re-layouts: 0.71 us -> 0 us
  Pallas kernels: 28.3 us -> 29 us
    pallas_call x0 -> x1, Pallas kernels: none -> 0.85 us  [shards(): pl.pallas_call(finish, out_shape=jax.ShapeDtypeStruct((8, 4, 16, 128), f3...]
    unnamed x1 -> x0, local copies, waits for them, and re-layouts: 0.71 us -> none
where the time goes in v6:
time: 29.2 us; the launch traced here: 29 us
  Pallas kernels  29 us (99%)
    pallas_call x1, Pallas kernels, shards(): pl.pallas_call(functools.partial(kernel, n_az, n_rad, 12 if n_az % 12 ==...  28.1 us
    pallas_call x1, Pallas kernels, shards(): pl.pallas_call(finish, out_shape=jax.ShapeDtypeStruct((8, 4, 16, 128), f3...  0.85 us

profile of v6, /device:TPU:1, one launch (start us, length us, event | category | flops | bytes accessed | tf_op | source)
XLA Modules:
  0.0 29.0 jit_solution(11811317834011034552)
XLA Ops:
  0.0 28.1 %shard_map.55 = (f32[8,4,16,128]{3,2,1,0:T(8,128)S(1)}, f32[8,16,128]{2,1,0:T(8,128)S(1)}) custom-call(s32[2]{0:T(128)} %off_hbm.1, f32[4,16,128]{2,1,0:T(8,128)} %den.1, f32[3,4,16,128]{3,2,1,0:T(8,128)} %mom.1, f32[3,4,16,128]{3,2,1,0:T(8,128)} %mag.1, f32[4,16,128]{2,1,0:T(8,128)} %tra.1), custom_call_target="tpu_custom_call" | custom-call | tf_op jit(solution)/shard_map/pallas_call | solution.py:496
  28.1 0.9 %shard_map.56 = f32[8,4,16,128]{3,2,1,0:T(8,128)} custom-call(f32[8,4,16,128]{3,2,1,0:T(8,128)S(1)} %get-tuple-element.7.pre, f32[8,16,128]{2,1,0:T(8,128)S(1)} %get-tuple-element.8.part), custom_call_target="tpu_custom_call" | custom-call | tf_op jit(solution)/shard_map/pallas_call | solution.py:523
